TPU v7x, 32 devices: a whole 2x2x4 slice. The times are simulated.
32 devices in a mesh: term: 8 (over z, x), sector: 4 (over y, core).
Axes of the slice: x: 2, y: 2, z: 4, core: 2. Of those that a mesh axis runs over, the one named last changes fastest.
Arguments:
- psi_start: float32 [4, 384, 384], P('sector'), may hold values from -6 to 6
- diagonal: float32 [4, 384, 384], P('sector'), may hold values from -3 to 3
- left_ops: float32 [128, 384, 384], P(('term', 'sector')), may hold values from -0.3125 to 0.3125
- right_ops: float32 [128, 384, 384], P(('term', 'sector')), may hold values from -0.078125 to 0.078125
- pair_in: int32 [32, 4], P(('term', 'sector')), may hold values from 0 to 3
- pair_out: int32 [32, 4], P(('term', 'sector')), may hold values from 0 to 3
- pair_count: int32 [32], P(('term', 'sector')), may hold values from 1 to 4, as said below
Outputs:
- psi_final: float32 [4, 384, 384], P('sector')
- energies: float32 [2], replicated
Inputs may be any that keep to these rules, and one draw needn't show every extreme that they name: `pair_count`: some device has all 4 slots live in every draw.
All inputs are finite; a program needn't handle non-finite values.
Results may differ from a plain program's by a relative error of at most 0.00013.
Values sent between devices are 32-bit elements; how exact they have to be, the bound alone decides.
No kernel may reach another device: no remote copies, remote signals or barrier semaphores. Data moves between devices by JAX's collectives and lax.ppermute only.
A program may use at most 64 MiB of HBM per device.

v0:
```python
import jax
import jax.numpy as jnp
from jax import lax
from jax.sharding import PartitionSpec as P

ITERS = 2
epsilon = 1e-06


def apply_pairs(gathered, left_ops, right_ops, pair_in, pair_out, pair_count):

    def one_pair(pair_slot, partial_value):
        source = lax.dynamic_index_in_dim(gathered, pair_in[0, pair_slot], 0, keepdims=False)
        left_block = lax.dynamic_index_in_dim(left_ops, pair_slot, 0, keepdims=False)
        right_block = lax.dynamic_index_in_dim(right_ops, pair_slot, 0, keepdims=False)
        inner_prod = jnp.dot(left_block, source, precision=lax.Precision.HIGHEST)
        product = lax.dot_general(
            inner_prod, right_block, (((1,), (1,)), ((), ())), precision=lax.Precision.HIGHEST
        )
        target = pair_out[0, pair_slot]
        current = lax.dynamic_index_in_dim(partial_value, target, 0, keepdims=False)
        return lax.dynamic_update_index_in_dim(partial_value, current + product, target, 0)

    return lax.fori_loop(0, pair_count[0], one_pair, jnp.zeros(gathered.shape, jnp.float32))


def global_sums(values):
    return lax.psum((values[0],), "sector")


def sigma_blocks(vector, left_ops, right_ops, pair_in, pair_out, pair_count):
    gathered = lax.all_gather(vector, "sector", axis=0, tiled=True)
    partial_value = apply_pairs(gathered, left_ops, right_ops, pair_in, pair_out, pair_count)
    owned_sum = lax.psum_scatter(partial_value, "sector", scatter_dimension=0, tiled=True)
    return lax.psum(owned_sum, "term")


def shards(psi_start, diagonal, left_ops, right_ops, pair_in, pair_out, pair_count):
    vector = psi_start
    cell_total = float(
        psi_start.shape[0] * lax.axis_size("sector") * psi_start.shape[1] * psi_start.shape[2]
    )
    energies = []
    for sweep in range(ITERS):
        vec_share = vector
        squares = global_sums((jnp.sum(vec_share * vec_share),))[0]
        inverse_norm = 1.0 / jnp.sqrt(squares / cell_total + epsilon)
        normed = vector * inverse_norm
        sigma = sigma_blocks(normed, left_ops, right_ops, pair_in, pair_out, pair_count)
        product_sum = global_sums((jnp.sum(normed * sigma),))[0]
        rayleigh = product_sum / cell_total
        residual = sigma - rayleigh * normed
        correction = residual / jnp.maximum(jnp.abs(diagonal - rayleigh), 1.0)
        updated = normed - correction
        vector = updated
        energies.append(rayleigh)
    return (vector, jnp.stack(energies))


def solution(mesh):
    return jax.shard_map(
        shards,
        mesh=mesh,
        in_specs=(
            P("sector", None, None),
            P("sector", None, None),
            P(("term", "sector"), None, None),
            P(("term", "sector"), None, None),
            P(("term", "sector"), None),
            P(("term", "sector"), None),
            P(("term", "sector")),
        ),
        out_specs=(P("sector", None, None), P()),
        check_vma=False,
    )
```

profile of v0, /device:TPU:0, one launch (start us, length us, event | category | flops | bytes accessed | tf_op | source)
XLA Modules:
  0.0 407.2 jit_solution(11676332899711747829)
XLA Ops:
  7.2 1.8 multiply_reduce_fusion.3
  9.1 9.0 %psum.42 = f32[]{:T(128)} all-reduce(f32[]{:T(128)} %multiply_reduce_fusion.3), channel_id=1, replica_groups=mesh['term'=8,'sector'=4] {'sector'}, use_global_device_ids=true, to_apply=%region_1.0 | all-reduce | flops 1 | bytes 8 | tf_op jit(solution)/shard_map/psum | solution.py:28
  18.7 1.9 broadcast_multiply_fusion.1
  20.7 24.4 %all-gather.3.cloned.1.call-done = f32[4,384,384]{2,1,0:T(8,128)} async-done(((f32[1,384,384]{2,1,0:T(8,128)}), f32[4,384,384]{2,1,0:T(8,128)}) %all-gather.3.cloned.1.call-update) | async-done | bytes 2359312 | tf_op jit(solution)/shard_map/all_gather | solution.py:32
  45.2 0.2 broadcast.6.clone
  45.4 39.8 %while.20 = (s32[]{:T(128)}, f32[4,384,384]{2,1,0:T(8,128)S(1)}, s32[]{:T(128)}, s32[1,4]{1,0:T(1,128)S(1)}, f32[4,384,384]{2,1,0:T(8,128)}, /*index=5*/s32[1,4]...) while((s32[]{:T(128)}, f32[4,384,384]{2,1,0:T(8,128)S(1)}, ...), condition=%wide.region_3.4_spmd, body=%wide.region_2.3_spmd.sunk | while | flops 1359101952 | bytes 5308675 | solution.py:24
  46.0 0.6 constant_dynamic-slice_fusion.10
  50.2 2.5 fusion.40
  52.8 2.3 fusion.41
  55.8 0.6 constant_dynamic-slice_fusion.10
  60.0 2.5 fusion.40
  62.6 2.3 fusion.41
  65.6 0.6 constant_dynamic-slice_fusion.10
  69.8 2.5 fusion.40
  72.4 2.3 fusion.41
  75.4 0.6 constant_dynamic-slice_fusion.10
  79.6 2.5 fusion.40
  82.1 2.3 fusion.41
  85.2 1.4 copy-done.1
  86.6 32.9 %reduce-scatter.3.cloned.1.call-done = f32[1,384,384]{2,1,0:T(8,128)} async-done(((f32[4,384,384]{2,1,0:T(8,128)}), f32[1,384,384]{2,1,0:T(8,128)}) %reduce-scatter.3.cloned.1.call-update) | async-done | bytes 589840 | tf_op jit(solution)/shard_map/reduce_scatter | solution.py:34
  119.6 76.6 %all-reduce.3.cloned.1.call-done = f32[1,384,384]{2,1,0:T(8,128)} async-done(((f32[1,384,384]{2,1,0:T(8,128)}), f32[1,384,384]{2,1,0:T(8,128)}) %all-reduce.3.cloned.1.call-update) | async-done | bytes 589840 | tf_op jit(solution)/shard_map/psum | solution.py:35
  196.2 1.8 multiply_reduce_fusion.2
  198.0 6.3 %psum.44 = f32[]{:T(128)} all-reduce(f32[]{:T(128)} %multiply_reduce_fusion.2), channel_id=1, replica_groups=mesh['term'=8,'sector'=4] {'sector'}, use_global_device_ids=true, to_apply=%region_7.8 | all-reduce | flops 1 | bytes 8 | tf_op jit(solution)/shard_map/psum | solution.py:28
  204.9 1.9 multiply_reduce_fusion.1
  206.8 7.2 %psum.45 = f32[]{:T(128)} all-reduce(f32[]{:T(128)} %get-tuple-element.122), channel_id=1, replica_groups=mesh['term'=8,'sector'=4] {'sector'}, use_global_device_ids=true, to_apply=%region_9.10 | all-reduce | flops 1 | bytes 8 | tf_op jit(solution)/shard_map/psum | solution.py:28
  214.7 0.9 broadcast_multiply_fusion
  215.7 22.5 %all-gather.5.cloned.1.call-done = f32[4,384,384]{2,1,0:T(8,128)} async-done(((f32[1,384,384]{2,1,0:T(8,128)}), f32[4,384,384]{2,1,0:T(8,128)}) %all-gather.5.cloned.1.call-update) | async-done | bytes 2359312 | tf_op jit(solution)/shard_map/all_gather | solution.py:32
  238.2 0.2 broadcast.6
  238.3 39.8 %while.21 = (s32[]{:T(128)}, f32[4,384,384]{2,1,0:T(8,128)S(1)}, s32[]{:T(128)}, s32[1,4]{1,0:T(1,128)S(1)}, f32[4,384,384]{2,1,0:T(8,128)}, /*index=5*/s32[1,4]...) while((s32[]{:T(128)}, f32[4,384,384]{2,1,0:T(8,128)S(1)}, ...), condition=%wide.region_11.12_spmd, body=%wide.region_10.11_spmd.sunk | while | flops 1359101952 | bytes 5308675 | solution.py:24
  239.0 0.6 constant_dynamic-slice_fusion.12
  243.2 2.5 fusion.46
  245.8 2.3 fusion.47
  248.8 0.6 constant_dynamic-slice_fusion.12
  253.0 2.5 fusion.46
  255.5 2.3 fusion.47
  258.6 0.6 constant_dynamic-slice_fusion.12
  262.8 2.5 fusion.46
  265.3 2.3 fusion.47
  268.3 0.6 constant_dynamic-slice_fusion.12
  272.5 2.5 fusion.46
  275.1 2.3 fusion.47
  278.1 1.4 copy-done
  279.6 32.9 %reduce-scatter.5.cloned.1.call-done = f32[1,384,384]{2,1,0:T(8,128)} async-done(((f32[4,384,384]{2,1,0:T(8,128)}), f32[1,384,384]{2,1,0:T(8,128)}) %reduce-scatter.5.cloned.1.call-update) | async-done | bytes 589840 | tf_op jit(solution)/shard_map/reduce_scatter | solution.py:34
  312.5 76.5 %all-reduce.5.cloned.1.call-done = f32[1,384,384]{2,1,0:T(8,128)} async-done(((f32[1,384,384]{2,1,0:T(8,128)}), f32[1,384,384]{2,1,0:T(8,128)}) %all-reduce.5.cloned.1.call-update) | async-done | bytes 589840 | tf_op jit(solution)/shard_map/psum | solution.py:35
  389.0 1.8 multiply_reduce_fusion
  390.8 6.3 %psum.47 = f32[]{:T(128)} all-reduce(f32[]{:T(128)} %multiply_reduce_fusion), channel_id=1, replica_groups=mesh['term'=8,'sector'=4] {'sector'}, use_global_device_ids=true, to_apply=%region_15.16 | all-reduce | flops 1 | bytes 8 | tf_op jit(solution)/shard_map/psum | solution.py:28
  397.8 0.6 pad_maximum_fusion
  398.3 2.1 divide_subtract_fusion
  (30 shorter events, 0.7 us)
Async XLA Ops:
  7.2 38.2 %copy-start.4 = (s32[1,4]{1,0:T(1,128)S(1)}, s32[1,4]{1,0:T(1,128)}, u32[]{:S(2)}) copy-start(s32[1,4]{1,0:T(1,128)} %param.16) | copy-start | bytes 52
  7.2 38.2 %copy-start.5 = (s32[1,4]{1,0:T(1,128)S(1)}, s32[1,4]{1,0:T(1,128)}, u32[]{:S(2)}) copy-start(s32[1,4]{1,0:T(1,128)} %param.15) | copy-start | bytes 52
  7.2 38.0 %all-gather.3.cloned.1.call-start = ((), (), s32[]{:S(2)}) async-start(), calls=%async_computation.2 | async-start | bytes 2949120 | tf_op jit(solution)/shard_map/all_gather | solution.py:32
  20.7 98.9 %reduce-scatter.3.cloned.1.call-start = ((), (), s32[]{:S(2)}) async-start(), calls=%async_computation.3 | async-start | bytes 2949120 | tf_op jit(solution)/shard_map/reduce_scatter | solution.py:34
  85.1 1.4 copy-start.1
  85.1 111.0 %copy-start.2 = (f32[1,384,384]{2,1,0:T(8,128)S(1)}, f32[1,384,384]{2,1,0:T(8,128)}, u32[]{:S(2)}) copy-start(f32[1,384,384]{2,1,0:T(8,128)} %param.11) | copy-start | bytes 1769476
  85.2 119.8 %copy-start.3 = (f32[1,384,384]{2,1,0:T(8,128)S(1)}, f32[1,384,384]{2,1,0:T(8,128)}, u32[]{:S(2)}) copy-start(f32[1,384,384]{2,1,0:T(8,128)} %param.12) | copy-start | bytes 1769476
  86.6 109.6 %all-reduce.3.cloned.1.call-start = ((), (), s32[]{:S(2)}) async-start(), calls=%async_computation.4 | async-start | bytes 1179648 | tf_op jit(solution)/shard_map/psum | solution.py:35
  119.6 118.6 %all-gather.5.cloned.1.call-start = ((), (), s32[]{:S(2)}) async-start(), calls=%async_computation.5 | async-start | bytes 2949120 | tf_op jit(solution)/shard_map/all_gather | solution.py:32
  215.6 96.9 %reduce-scatter.5.cloned.1.call-start = ((), (), s32[]{:S(2)}) async-start(), calls=%async_computation.6 | async-start | bytes 2949120 | tf_op jit(solution)/shard_map/reduce_scatter | solution.py:34
  278.1 1.4 copy-start
  279.5 109.5 %all-reduce.5.cloned.1.call-start = ((), (), s32[]{:S(2)}) async-start(), calls=%async_computation.7 | async-start | bytes 1179648 | tf_op jit(solution)/shard_map/psum | solution.py:35
Sparse Core Ops, SparseCore 0:
  20.8 24.3 all-gather.2
  86.7 32.8 reduce-scatter.2
  122.9 73.2 all-reduce.2
  215.7 22.4 all-gather.4
  279.7 32.8 reduce-scatter.4
  315.7 73.2 all-reduce.4
where the time goes:
time: 409 us; the launch traced here: 407 us
  waiting for transfers between devices  266 us (65%)
  matrix products  38.7 us (9%)
  loops' own time  35.8 us (9%)
  blocking collectives  28.7 us (7%)
  between operations  16.9 us (4%)
  other arithmetic  12.8 us (3%)
  local copies, waits for them, and re-layouts  8.2 us (2%)
    psum x2, waiting for transfers between devices, sigma_blocks(): return lax.psum(owned_sum, 'term')  153 us
    reduce_scatter x2, waiting for transfers between devices, sigma_blocks(): lax.psum_scatter(partial_value, 'sector', scatter_dimension=0, tiled=True)  65.8 us
    all_gather x2, waiting for transfers between devices, sigma_blocks(): gathered = lax.all_gather(vector, 'sector', axis=0, tiled=True)  47 us
    another operation x2, loops' own time, apply_pairs(): lax.fori_loop(0, pair_count[0], one_pair, jnp.zeros(gathered.shape, jnp.f...  35.8 us
    psum x4, blocking collectives, global_sums(): return lax.psum((values[0],), 'sector')  28.7 us
    dot_general x8, matrix products, one_pair(): inner_prod = jnp.dot(left_block, source, precision=lax.Precision.HIGHEST)  20 us
    dot_general x8, matrix products, one_pair(): lax.dot_general(inner_prod, right_block, (((1,), (1,)), ((), ())), precis...  18.6 us
  transfers between devices with their start and end apart: 6, of which 6 were waited for; matrix products, arithmetic and copies ran while one was open for 0% of the time, Pallas kernels for 0%

commit v1 on v0

--- a/solution.py
+++ b/solution.py
@@ -29,7 +29,16 @@
 
 
 def sigma_blocks(vector, left_ops, right_ops, pair_in, pair_out, pair_count):
-    gathered = lax.all_gather(vector, "sector", axis=0, tiled=True)
+    even = jax.lax.axis_size("sector")
+    before, x_new = (even, jax.lax.axis_index("sector"))
+    gathered, arr_out = (vector, 1)
+    while arr_out < before:
+        y2 = tuple(((dev_j, dev_j ^ arr_out) for dev_j in range(before)))
+        b_now = jax.lax.ppermute(gathered, axis_name="sector", perm=y2)
+        placed = jnp.concatenate([gathered, b_now], axis=0)
+        upper = jnp.concatenate([b_now, gathered], axis=0)
+        gathered = jnp.where(x_new & arr_out == 0, placed, upper)
+        arr_out = 2 * arr_out
     partial_value = apply_pairs(gathered, left_ops, right_ops, pair_in, pair_out, pair_count)
     owned_sum = lax.psum_scatter(partial_value, "sector", scatter_dimension=0, tiled=True)
     return lax.psum(owned_sum, "term")

time: 409 us -> 422 us (1.032)
  waiting for transfers between devices: 266 us -> 276 us
    ppermute x0 -> x4, waiting for transfers between devices: none -> 58.7 us  [sigma_blocks(): b_now = jax.lax.ppermute(gathered, axis_name='sector', perm=y2)]
    all_gather x2 -> x0, waiting for transfers between devices: 47 us -> none  [sigma_blocks(): gathered = lax.all_gather(vector, 'sector', axis=0, tiled=True)]
  transfers between devices with their start and end apart: 6 -> 8, of which waited for: 6 -> 8; matrix products, arithmetic and copies ran while one was open for 0% -> 0% of each run, Pallas kernels for 0% -> 0%
where the time goes in v1:
time: 422 us; the launch traced here: 421 us
  waiting for transfers between devices  276 us (65%)
  matrix products  38.7 us (9%)
  loops' own time  35.5 us (8%)
  blocking collectives  28.7 us (7%)
  between operations  16.6 us (4%)
  other arithmetic  14.6 us (3%)
  local copies, waits for them, and re-layouts  8.76 us (2%)
    psum x2, waiting for transfers between devices, sigma_blocks(): return lax.psum(owned_sum, 'term')  153 us
    reduce_scatter x2, waiting for transfers between devices, sigma_blocks(): lax.psum_scatter(partial_value, 'sector', scatter_dimension=0, tiled=True)  64.3 us
    ppermute x4, waiting for transfers between devices, sigma_blocks(): b_now = jax.lax.ppermute(gathered, axis_name='sector', perm=y2)  58.7 us
    another operation x2, loops' own time, apply_pairs(): lax.fori_loop(0, pair_count[0], one_pair, jnp.zeros(gathered.shape, jnp.f...  35.5 us
    psum x4, blocking collectives, global_sums(): return lax.psum((values[0],), 'sector')  28.7 us
    dot_general x8, matrix products, one_pair(): inner_prod = jnp.dot(left_block, source, precision=lax.Precision.HIGHEST)  20 us
    dot_general x8, matrix products, one_pair(): lax.dot_general(inner_prod, right_block, (((1,), (1,)), ((), ())), precis...  18.6 us
  transfers between devices with their start and end apart: 8, of which 8 were waited for; matrix products, arithmetic and copies ran while one was open for 0% of the time, Pallas kernels for 0%

profile of v1, /device:TPU:0, one launch (start us, length us, event | category | flops | bytes accessed | tf_op | source)
XLA Modules:
  0.0 420.7 jit_solution(7416440675835193257)
XLA Ops:
  7.2 1.8 multiply_reduce_fusion.3
  9.0 9.0 %psum.42 = f32[]{:T(128)} all-reduce(f32[]{:T(128)} %multiply_reduce_fusion.3), channel_id=1, replica_groups=mesh['term'=8,'sector'=4] {'sector'}, use_global_device_ids=true, to_apply=%region_1.0 | all-reduce | flops 1 | bytes 8 | tf_op jit(solution)/shard_map/psum | solution.py:28
  18.7 1.1 broadcast_multiply_fusion.1
  19.9 2.0 collective-permute-done
  22.4 27.6 %collective-permute-done.1 = f32[2,384,384]{2,1,0:T(8,128)S(1)} collective-permute-done((f32[2,384,384]{2,1,0:T(8,128)S(1)}, f32[2,384,384]{2,1,0:T(8,128)S(1)}, u32[]{:S(2)}, u32[]{:S(2)}) %collective-permute-start.1) | collective-permute-done | bytes 1179680 | tf_op jit(solution)/shard_map/ppermute | solution.py:37
  50.1 1.6 maximum_select_fusion
  52.3 39.8 %while.20 = (s32[]{:T(128)}, f32[4,384,384]{2,1,0:T(8,128)S(1)}, s32[]{:T(128)}, s32[1,4]{1,0:T(1,128)S(1)}, f32[4,384,384]{2,1,0:T(8,128)}, /*index=5*/s32[1,4]...) while((s32[]{:T(128)}, f32[4,384,384]{2,1,0:T(8,128)S(1)}, ...), condition=%wide.region_3.4_spmd, body=%wide.region_2.3_spmd.sunk | while | flops 1359101952 | bytes 5308675 | solution.py:24
  53.0 0.6 constant_dynamic-slice_fusion.10
  57.2 2.5 fusion.40
  59.7 2.3 fusion.41
  62.7 0.6 constant_dynamic-slice_fusion.10
  67.0 2.5 fusion.40
  69.5 2.3 fusion.41
  76.7 2.5 fusion.40
  79.3 2.3 fusion.41
  86.5 2.5 fusion.40
  89.1 2.3 fusion.41
  92.1 1.4 copy-done.1
  93.5 33.2 %reduce-scatter.3.cloned.1.call-done = f32[1,384,384]{2,1,0:T(8,128)} async-done(((f32[4,384,384]{2,1,0:T(8,128)}), f32[1,384,384]{2,1,0:T(8,128)}) %reduce-scatter.3.cloned.1.call-update) | async-done | bytes 589840 | tf_op jit(solution)/shard_map/reduce_scatter | solution.py:43
  126.8 76.6 %all-reduce.3.cloned.1.call-done = f32[1,384,384]{2,1,0:T(8,128)} async-done(((f32[1,384,384]{2,1,0:T(8,128)}), f32[1,384,384]{2,1,0:T(8,128)}) %all-reduce.3.cloned.1.call-update) | async-done | bytes 589840 | tf_op jit(solution)/shard_map/psum | solution.py:44
  203.4 1.8 multiply_reduce_fusion.2
  205.2 6.3 %psum.44 = f32[]{:T(128)} all-reduce(f32[]{:T(128)} %multiply_reduce_fusion.2), channel_id=1, replica_groups=mesh['term'=8,'sector'=4] {'sector'}, use_global_device_ids=true, to_apply=%region_7.8 | all-reduce | flops 1 | bytes 8 | tf_op jit(solution)/shard_map/psum | solution.py:28
  212.1 2.1 multiply_reduce_fusion.1
  214.2 7.2 %psum.45 = f32[]{:T(128)} all-reduce(f32[]{:T(128)} %get-tuple-element.122), channel_id=1, replica_groups=mesh['term'=8,'sector'=4] {'sector'}, use_global_device_ids=true, to_apply=%region_9.10 | all-reduce | flops 1 | bytes 8 | tf_op jit(solution)/shard_map/psum | solution.py:28
  222.2 2.0 collective-permute-done.2
  224.3 1.0 collective-permute-start.3
  225.3 27.1 %collective-permute-done.3 = f32[2,384,384]{2,1,0:T(8,128)S(1)} collective-permute-done((f32[2,384,384]{2,1,0:T(8,128)S(1)}, f32[2,384,384]{2,1,0:T(8,128)S(1)}, u32[]{:S(2)}, u32[]{:S(2)}) %collective-permute-start.3) | collective-permute-done | bytes 1179680 | tf_op jit(solution)/shard_map/ppermute | solution.py:37
  252.4 1.6 maximum_select_fusion.1
  254.1 39.5 %while.21 = (s32[]{:T(128)}, f32[4,384,384]{2,1,0:T(8,128)S(1)}, s32[]{:T(128)}, s32[1,4]{1,0:T(1,128)S(1)}, f32[4,384,384]{2,1,0:T(8,128)}, /*index=5*/s32[1,4]...) while((s32[]{:T(128)}, f32[4,384,384]{2,1,0:T(8,128)S(1)}, ...), condition=%wide.region_11.12_spmd, body=%wide.region_10.11_spmd.sunk | while | flops 1359101952 | bytes 5308675 | solution.py:24
  254.8 0.6 constant_dynamic-slice_fusion.12
  258.9 2.5 fusion.46
  261.5 2.3 fusion.47
  264.5 0.6 constant_dynamic-slice_fusion.12
  268.7 2.5 fusion.46
  271.2 2.3 fusion.47
  274.2 0.6 constant_dynamic-slice_fusion.12
  278.4 2.5 fusion.46
  280.9 2.3 fusion.47
  283.9 0.6 constant_dynamic-slice_fusion.12
  288.1 2.5 fusion.46
  290.7 2.3 fusion.47
  293.7 1.4 copy-done
  295.1 31.1 %reduce-scatter.5.cloned.1.call-done = f32[1,384,384]{2,1,0:T(8,128)} async-done(((f32[4,384,384]{2,1,0:T(8,128)}), f32[1,384,384]{2,1,0:T(8,128)}) %reduce-scatter.5.cloned.1.call-update) | async-done | bytes 589840 | tf_op jit(solution)/shard_map/reduce_scatter | solution.py:43
  326.3 76.5 %all-reduce.5.cloned.1.call-done = f32[1,384,384]{2,1,0:T(8,128)} async-done(((f32[1,384,384]{2,1,0:T(8,128)}), f32[1,384,384]{2,1,0:T(8,128)}) %all-reduce.5.cloned.1.call-update) | async-done | bytes 589840 | tf_op jit(solution)/shard_map/psum | solution.py:44
  402.8 1.8 multiply_reduce_fusion
  404.6 6.3 %psum.47 = f32[]{:T(128)} all-reduce(f32[]{:T(128)} %multiply_reduce_fusion), channel_id=1, replica_groups=mesh['term'=8,'sector'=4] {'sector'}, use_global_device_ids=true, to_apply=%region_15.16 | all-reduce | flops 1 | bytes 8 | tf_op jit(solution)/shard_map/psum | solution.py:28
  411.5 0.6 pad_maximum_fusion
  412.1 2.1 divide_subtract_fusion
  (36 shorter events, 3.4 us)
Async XLA Ops:
  7.2 119.6 %reduce-scatter.3.cloned.1.call-start = ((), (), s32[]{:S(2)}) async-start(), calls=%async_computation.2 | async-start | bytes 2949120 | tf_op jit(solution)/shard_map/reduce_scatter | solution.py:43
  19.8 2.1 collective-permute-start
  22.0 28.1 %collective-permute-start.1 = (f32[2,384,384]{2,1,0:T(8,128)S(1)}, f32[2,384,384]{2,1,0:T(8,128)S(1)}, u32[]{:S(2)}, u32[]{:S(2)}) collective-permute-start(f32[2,384,384]{2,1,0:T(8,128)S(1)} %maximum_select_fusion.2), channel_id=1, source_target_pairs={{0,2},{1,3},{2,0},{3,1},{4,6},{5,7},{6,4},{7,5},{8,10},{9,11},{10,... | collective-permute-start | bytes 3538952 | tf_op jit(solution)/shard_map/ppermute | solution.py:37
  51.6 0.7 copy-start.4
  51.6 0.7 copy-start.5
  92.1 1.4 copy-start.1
  92.1 111.3 %copy-start.2 = (f32[1,384,384]{2,1,0:T(8,128)S(1)}, f32[1,384,384]{2,1,0:T(8,128)}, u32[]{:S(2)}) copy-start(f32[1,384,384]{2,1,0:T(8,128)} %param.11) | copy-start | bytes 1769476
  93.5 109.9 %all-reduce.3.cloned.1.call-start = ((), (), s32[]{:S(2)}) async-start(), calls=%async_computation.3 | async-start | bytes 1179648 | tf_op jit(solution)/shard_map/psum | solution.py:44
  126.8 199.5 %reduce-scatter.5.cloned.1.call-start = ((), (), s32[]{:S(2)}) async-start(), calls=%async_computation.4 | async-start | bytes 2949120 | tf_op jit(solution)/shard_map/reduce_scatter | solution.py:43
  222.2 2.1 collective-permute-start.2
  224.3 28.1 %collective-permute-start.3 = (f32[2,384,384]{2,1,0:T(8,128)S(1)}, f32[2,384,384]{2,1,0:T(8,128)S(1)}, u32[]{:S(2)}, u32[]{:S(2)}) collective-permute-start(f32[2,384,384]{2,1,0:T(8,128)S(1)} %maximum_select_fusion.3), channel_id=1, source_target_pairs={{0,2},{1,3},{2,0},{3,1},{4,6},{5,7},{6,4},{7,5},{8,10},{9,11},{10,... | collective-permute-start | bytes 3538952 | tf_op jit(solution)/shard_map/ppermute | solution.py:37
  293.7 1.4 copy-start
  293.7 118.5 %copy-start.3 = (f32[1,384,384]{2,1,0:T(8,128)S(1)}, f32[1,384,384]{2,1,0:T(8,128)}, u32[]{:S(2)}) copy-start(f32[1,384,384]{2,1,0:T(8,128)} %param.12) | copy-start | bytes 1769476
  295.1 107.7 %all-reduce.5.cloned.1.call-start = ((), (), s32[]{:S(2)}) async-start(), calls=%async_computation.5 | async-start | bytes 1179648 | tf_op jit(solution)/shard_map/psum | solution.py:44
Sparse Core Ops, SparseCore 0:
  93.6 33.0 reduce-scatter.2
  130.1 73.2 all-reduce.2
  295.2 31.0 reduce-scatter.4
  329.5 73.2 all-reduce.4
